TPU v7x, 32 devices: a whole 2x2x4 slice. The times are simulated.
32 devices in a mesh: row: 8 (over z, core), col: 4 (over y, x).
Axes of the slice: x: 2, y: 2, z: 4, core: 2. Of those that a mesh axis runs over, the one named last changes fastest.
Arguments:
- iterate: bfloat16 [3584, 18432], P('col', 'row'), may hold values from -5.2 to 5.2
Outputs:
- next_iterate: float32 [3584, 18432], P('col', 'row')
All inputs are finite; a program needn't handle non-finite values.
Results may differ from a plain program's by a relative error of at most 0.0032.
Values may be sent and summed in bfloat16 or wider, within the bound.
A program may use at most 128 MiB of HBM per device.

v0:
```python
import jax
import jax.numpy as jnp
from jax import lax
from jax.sharding import PartitionSpec as P

N = 18432


QUINTIC_A = 3.4445
QUINTIC_B = -4.775
QUINTIC_C = 2.0315


def local(iterate):
    inverse = 1.0 / N
    column_slab = lax.all_gather(iterate, "col", axis=0, tiled=True)
    gram_total = lax.psum_scatter(
        lax.dot_general(
            column_slab, iterate, (((1,), (1,)), ((), ())), preferred_element_type=jnp.float32
        ),
        "row",
        scatter_dimension=0,
        tiled=True,
    )
    gram_tile = (gram_total * inverse).astype(jnp.bfloat16)
    row_panel = lax.all_gather(gram_tile, "col", axis=1, tiled=True)
    square = jnp.dot(
        row_panel,
        lax.all_gather(gram_tile, "row", axis=0, tiled=True),
        preferred_element_type=jnp.float32,
    )
    poly_tile = (QUINTIC_B * gram_tile.astype(jnp.float32) + QUINTIC_C * square).astype(
        jnp.bfloat16
    )
    product = lax.dot_general(
        lax.all_gather(poly_tile, "row", axis=0, tiled=True),
        column_slab,
        (((0,), (0,)), ((), ())),
        preferred_element_type=jnp.float32,
    )
    return QUINTIC_A * iterate.astype(jnp.float32) + product


def solution(mesh):
    placed = (P("col", "row"),)
    return jax.shard_map(
        local, mesh=mesh, in_specs=placed, out_specs=P("col", "row"), check_vma=False
    )
```

profile of v0, /device:TPU:0, one launch (start us, length us, event | category | flops | bytes accessed | tf_op | source)
XLA Modules:
  0.0 536.6 jit_solution(12580601077064805445)
XLA Ops:
  6.5 0.0 all-gather.5.cloned.1.call-start
  6.5 0.7 all-gather.5.cloned.1.call-update
  7.3 0.0 reduce-scatter.2.cloned.1.call-start
  7.3 159.9 %all-gather.5.cloned.1.call-done = bf16[3584,2304]{1,0:T(8,128)(2,1)} async-done(((bf16[896,2304]{1,0:T(8,128)(2,1)}), bf16[3584,2304]{1,0:T(8,128)(2,1)}) %all-gather.5.cloned.1.call-update) | async-done | bytes 16515088 | tf_op jit(solution)/shard_map/all_gather | solution.py:16
  167.2 22.9 %fusion = f32[3584,896]{1,0:T(8,128)} fusion(bf16[3584,2304]{1,0:T(8,128)(2,1)} %all-gather.5.cloned.1.call-done, bf16[896,2304]{1,0:T(8,128)(2,1)} %param.1), kind=kOutput, calls=%fused_computation.3 | convolution fusion | flops 14797504512 | bytes 33488896 | tf_op jit(solution)/shard_map/dot_general | solution.py:18
  190.1 0.0 reduce-scatter.2.cloned.1.call-update
  190.1 0.0 all-gather.7.cloned.1.call-start
  190.2 131.8 %reduce-scatter.2.cloned.1.call-done = f32[448,896]{1,0:T(8,128)} async-done(((f32[3584,896]{1,0:T(8,128)}), f32[448,896]{1,0:T(8,128)}) %reduce-scatter.2.cloned.1.call-update) | async-done | bytes 1605648 | tf_op jit(solution)/shard_map/reduce_scatter | solution.py:17
  322.0 2.4 multiply_convert_fusion
  324.4 0.0 all-gather.7.cloned.1.call-update
  324.4 0.0 all-gather.9.cloned.1.call-start
  324.5 0.5 all-gather.9.cloned.1.call-update
  325.0 0.0 all-gather.11.cloned.1.call-start
  325.0 42.4 %all-gather.7.cloned.1.call-done = bf16[448,3584]{1,0:T(8,128)(2,1)} async-done(((bf16[448,896]{1,0:T(8,128)(2,1)}), bf16[448,3584]{1,0:T(8,128)(2,1)}) %all-gather.7.cloned.1.call-update) | async-done | bytes 3211280 | tf_op jit(solution)/shard_map/all_gather | solution.py:26
  367.5 67.4 %all-gather.9.cloned.1.call-done = bf16[3584,896]{1,0:T(8,128)(2,1)} async-done(((bf16[448,896]{1,0:T(8,128)(2,1)}), bf16[3584,896]{1,0:T(8,128)(2,1)}) %all-gather.9.cloned.1.call-update) | async-done | bytes 6422544 | tf_op jit(solution)/shard_map/all_gather | solution.py:29
  434.8 8.3 %add_convert_fusion = bf16[448,896]{1,0:T(8,128)(2,1)} fusion(bf16[448,896]{1,0:T(8,128)(2,1)} %multiply_convert_fusion, bf16[448,3584]{1,0:T(8,128)(2,1)} %all-gather.7.cloned.1.call-done, bf16[3584,896]{1,0:T(8,128)(2,1)} %all-gather.9.cloned.1.call-done), kind=kOutput, calls=%fused_computation.1 | convolution fusion | flops 2879299584 | bytes 11239424 | tf_op jit(solution)/shard_map/dot_general | solution.py:27
  443.1 0.0 all-gather.11.cloned.1.call-update
  443.1 64.6 %all-gather.11.cloned.1.call-done = bf16[3584,896]{1,0:T(8,128)(2,1)} async-done(((bf16[448,896]{1,0:T(8,128)(2,1)}), bf16[3584,896]{1,0:T(8,128)(2,1)}) %all-gather.11.cloned.1.call-update) | async-done | bytes 6422544 | tf_op jit(solution)/shard_map/all_gather | solution.py:36
  507.8 22.3 %multiply_add_fusion = f32[896,2304]{1,0:T(8,128)} fusion(bf16[896,2304]{1,0:T(8,128)(2,1)} %param.1, bf16[3584,896]{1,0:T(8,128)(2,1)} %all-gather.11.cloned.1.call-done, bf16[3584,2304]{1,0:T(8,128)(2,1)} %all-gather.5.cloned.1.call-done), kind=kOutput, calls=%fused_computation | convolution fusion | flops 14803697664 | bytes 35323904 | tf_op jit(solution)/shard_map/dot_general | solution.py:35
Async XLA Ops:
  6.5 160.6 %all-gather.5.cloned.1.call-start = ((), (), s32[]{:S(2)}) async-start(), calls=%async_computation.1 | async-start | bytes 20643840 | tf_op jit(solution)/shard_map/all_gather | solution.py:16
  7.3 314.7 %reduce-scatter.2.cloned.1.call-start = ((), (), s32[]{:S(2)}) async-start(), calls=%async_computation.2 | async-start | bytes 14450688 | tf_op jit(solution)/shard_map/reduce_scatter | solution.py:17
  190.1 177.4 %all-gather.7.cloned.1.call-start = ((), (), s32[]{:S(2)}) async-start(), calls=%async_computation.3 | async-start | bytes 4014080 | tf_op jit(solution)/shard_map/all_gather | solution.py:26
  324.4 110.4 %all-gather.9.cloned.1.call-start = ((), (), s32[]{:S(2)}) async-start(), calls=%async_computation.4 | async-start | bytes 7225344 | tf_op jit(solution)/shard_map/all_gather | solution.py:29
  325.0 182.8 %all-gather.11.cloned.1.call-start = ((), (), s32[]{:S(2)}) async-start(), calls=%async_computation.5 | async-start | bytes 7225344 | tf_op jit(solution)/shard_map/all_gather | solution.py:36
Sparse Core Ops, SparseCore 0:
  9.2 157.9 all-gather.4
  190.2 131.6 reduce-scatter.1
  324.5 42.8 all-gather.6
  369.0 65.8 all-gather.8
  443.2 64.4 all-gather.10
where the time goes:
time: 537 us
  waiting for transfers between devices  467 us (87%)
  matrix products  53.4 us (10%)
  between operations  13.1 us (2%)
    all_gather x1, waiting for transfers between devices, local(): column_slab = lax.all_gather(iterate, 'col', axis=0, tiled=True)  160 us
    reduce_scatter x1, waiting for transfers between devices, local(): lax.psum_scatter(lax.dot_general(column_slab, iterate, (((1,), (1,)), (()...  132 us
    all_gather x1, waiting for transfers between devices, local(): lax.all_gather(gram_tile, 'row', axis=0, tiled=True)  67.4 us
    all_gather x1, waiting for transfers between devices, local(): lax.all_gather(poly_tile, 'row', axis=0, tiled=True)  64.6 us
    all_gather x1, waiting for transfers between devices, local(): row_panel = lax.all_gather(gram_tile, 'col', axis=1, tiled=True)  42.4 us
    dot_general x1, matrix products, local(): lax.dot_general(column_slab, iterate, (((1,), (1,)), ((), ())), preferred...  22.9 us
    dot_general x1, matrix products, local(): lax.dot_general(lax.all_gather(poly_tile, 'row', axis=0, tiled=True), col...  22.3 us
  transfers between devices with their start and end apart: 5, of which 5 were waited for; matrix products, arithmetic and copies ran while one was open for 0% of the time, Pallas kernels for 0%

commit v1 on v0

v1 whole, which is shorter than its diff:
```python
import functools

import jax
import jax.numpy as jnp
from jax import lax
from jax.experimental import pallas as pl
from jax.experimental.pallas import tpu as pltpu
from jax.sharding import PartitionSpec as P

N = 18432


QUINTIC_A = 3.4445
QUINTIC_B = -4.775
QUINTIC_C = 2.0315

VMEM_LIMIT = 60 * 2**20
ROWS_BY_ROWS = (((1,), (1,)), ((), ()))
COLS_BY_ROWS = (((0,), (0,)), ((), ()))


def general(iterate):
    inverse = 1.0 / N
    column_slab = lax.all_gather(iterate, "col", axis=0, tiled=True)
    gram_total = lax.psum_scatter(
        lax.dot_general(column_slab, iterate, ROWS_BY_ROWS, preferred_element_type=jnp.float32),
        "row",
        scatter_dimension=0,
        tiled=True,
    )
    gram_tile = (gram_total * inverse).astype(jnp.bfloat16)
    row_panel = lax.all_gather(gram_tile, "col", axis=1, tiled=True)
    square = jnp.dot(
        row_panel,
        lax.all_gather(gram_tile, "row", axis=0, tiled=True),
        preferred_element_type=jnp.float32,
    )
    poly_tile = (QUINTIC_B * gram_tile.astype(jnp.float32) + QUINTIC_C * square).astype(
        jnp.bfloat16
    )
    product = lax.dot_general(
        lax.all_gather(poly_tile, "row", axis=0, tiled=True),
        column_slab,
        COLS_BY_ROWS,
        preferred_element_type=jnp.float32,
    )
    return QUINTIC_A * iterate.astype(jnp.float32) + product


def polynomial_kernel(
    depth, inverse, x_ref, slab_out, poly_out,
    slab, part, paired, outgoing, incoming, gram, panel, poly,
    x_send, x_recv, pair_send, pair_recv, sum_send, sum_recv,
    hop_send, hop_recv, side_send, side_recv, panel_send, panel_recv, out_sem,
):
    m = x_ref.shape[0]
    h, s = m // 2, m // (2 * depth)
    c, r = lax.axis_index("col"), lax.axis_index("row")
    z = r // 2
    core = r % 2
    side = r + 1 - 2 * core
    across = {1: c + 1 - 2 * (c % 2), 2: (c + 2) % 4, 3: 3 - c}
    lo, hi = pl.ds(0, h), pl.ds(h, h)

    def remote(source, target, send, recv, row=r, col=c):
        return pltpu.make_async_remote_copy(
            src_ref=source, dst_ref=target, send_sem=send, recv_sem=recv,
            device_id={"row": row, "col": col}, device_id_type=pl.DeviceIdType.MESH,
        )

    barrier = pltpu.get_barrier_semaphore()
    partners = [(r, across[l]) for l in (1, 2, 3)] + [(side, c)]
    partners += [(2 * ((z + d) % depth) + core, c) for d in range(1, depth)]
    for row, col in partners:
        pl.semaphore_signal(
            barrier, inc=1, device_id={"row": row, "col": col},
            device_id_type=pl.DeviceIdType.MESH,
        )
    pl.semaphore_wait(barrier, len(partners))

    def x_copy(i):
        source, block, half, bit = [
            (x_ref, 0, lo, 1),
            (x_ref, 1, hi, 2),
            (x_ref, 0, hi, 1),
            (x_ref, 1, lo, 2),
            (slab.at[0], 2, lo, 2),
            (slab.at[1], 2, hi, 1),
        ][i]
        return remote(
            source.at[half], slab.at[block, half], x_send.at[i], x_recv.at[i], col=across[bit]
        )

    def keep(k):
        source = x_ref if k == 0 else slab.at[k - 1]
        return pltpu.make_async_copy(source, slab_out.at[k], out_sem.at[k])

    def pair_copy(k):
        return remote(
            part.at[k % 2, 1 - core], paired.at[k], pair_send.at[k], pair_recv.at[k], row=side
        )

    def products(k):
        def step(i, carry):
            rows = pl.ds(pl.multiple_of(i * 2 * s, 2 * s), 2 * s)
            block = x_ref[rows] if k == 0 else slab[k - 1, rows]
            total = inverse * lax.dot_general(
                block, x_ref[...], ROWS_BY_ROWS, preferred_element_type=jnp.float32
            )
            part[k % 2, 0, i] = total[:s]
            part[k % 2, 1, i] = total[s:]
            return carry

        lax.fori_loop(0, depth, step, 0)
        pair_copy(k).start()

    def sum_copy(k, d):
        there = (z + d) % depth
        return remote(
            outgoing.at[k, there], incoming.at[k, d - 1],
            sum_send.at[k, d - 1], sum_recv.at[k, d - 1], row=2 * there + core,
        )

    def send_sums(k):
        pair_copy(k).wait_recv()

        def step(i, carry):
            outgoing[k, i] = (part[k % 2, core, i] + paired[k, i]).astype(jnp.bfloat16)
            return carry

        lax.fori_loop(0, depth, step, 0)
        for d in range(1, depth):
            sum_copy(k, d).start()

    def panel_copy(k, l):
        return remote(
            gram.at[k, r], panel.at[l, k ^ l],
            panel_send.at[k, l - 1], panel_recv.at[k, l - 1], col=across[l],
        )

    def finish_sums(k):
        total = part[k % 2, core, z] + paired[k, z]
        for d in range(1, depth):
            sum_copy(k, d).wait_recv()
            total += incoming[k, d - 1].astype(jnp.float32)
        total = total.astype(jnp.bfloat16)
        gram[k, r] = total
        panel[0, k] = total
        spread(0, gram, k)
        for l in (1, 2, 3):
            panel_copy(k, l).start()

    def hop(g, buffer, k, way, d):
        source = r - 2 * (d - 1) if way == 0 else r + 2 * (d - 1)
        target = r + 2 if way == 0 else r - 2
        return remote(
            buffer.at[k, source], buffer.at[k, source],
            hop_send.at[g, k, way, d - 1], hop_recv.at[g, k, way, d - 1], row=target,
        )

    def sends(way, d):
        if way == 0:
            return jnp.logical_and(z - (d - 1) >= 0, z <= depth - 2)
        return jnp.logical_and(z + (d - 1) <= depth - 1, z >= 1)

    def gets(way, d):
        return z - d >= 0 if way == 0 else z + d <= depth - 1

    def side_copy(g, buffer, k, way, d):
        source = r - 2 * d if way == 0 else r + 2 * d
        slot = d if way == 0 else depth - 1 + d
        return remote(
            buffer.at[k, source], buffer.at[k, source],
            side_send.at[g, k, slot], side_recv.at[g, k, slot], row=side,
        )

    def side_arrival(g, buffer, k, way, d):
        source = side - 2 * d if way == 0 else side + 2 * d
        slot = d if way == 0 else depth - 1 + d
        return remote(
            buffer.at[k, source], buffer.at[k, source],
            side_send.at[g, k, slot], side_recv.at[g, k, slot], row=side,
        )

    def arrival(g, buffer, k, way, d):
        source = r - 2 * d if way == 0 else r + 2 * d
        return remote(
            buffer.at[k, source], buffer.at[k, source],
            hop_send.at[g, k, way, d - 1], hop_recv.at[g, k, way, d - 1], row=side,
        )

    def spread(g, buffer, k):
        for way in (0, 1):
            pl.when(sends(way, 1))(lambda way=way: hop(g, buffer, k, way, 1).start())
        side_copy(g, buffer, k, 0, 0).start()

    def pass_on(g, buffer, k, d):
        for way in (0, 1):

            @pl.when(gets(way, d))
            def _(way=way):
                arrival(g, buffer, k, way, d).wait_recv()
                side_copy(g, buffer, k, way, d).start()

            if d < depth - 1:
                pl.when(sends(way, d + 1))(lambda way=way: hop(g, buffer, k, way, d + 1).start())

    def gathered(g, buffer, k):
        side_arrival(g, buffer, k, 0, 0).wait_recv()
        for way in (0, 1):
            for d in range(1, depth):
                pl.when(gets(way, d))(
                    lambda way=way, d=d: side_arrival(g, buffer, k, way, d).wait_recv()
                )

    def spread_sent(g, buffer, k):
        side_copy(g, buffer, k, 0, 0).wait_send()
        for way in (0, 1):
            for d in range(1, depth):
                pl.when(gets(way, d))(
                    lambda way=way, d=d: side_copy(g, buffer, k, way, d).wait_send()
                )
                pl.when(sends(way, d))(
                    lambda way=way, d=d: hop(g, buffer, k, way, d).wait_send()
                )

    x_copy(0).start()
    x_copy(1).start()
    keep(0).start()
    products(0)
    send_sums(0)
    for i in (0, 1):
        x_copy(i).wait()
    x_copy(2).start()
    x_copy(3).start()
    finish_sums(0)
    for d in range(1, depth):
        pass_on(0, gram, 0, d)
    for i in (2, 3):
        x_copy(i).wait()
    x_copy(4).start()
    x_copy(5).start()
    keep(1).start()
    keep(2).start()
    products(1)
    pair_copy(0).wait_send()
    products(2)
    send_sums(1)
    send_sums(2)
    finish_sums(1)
    finish_sums(2)
    for d in range(1, depth):
        pass_on(0, gram, 1, d)
        pass_on(0, gram, 2, d)
    pair_copy(1).wait_send()
    for i in (4, 5):
        x_copy(i).wait()
    keep(3).start()
    products(3)
    send_sums(3)
    finish_sums(3)
    for d in range(1, depth):
        pass_on(0, gram, 3, d)
    for k in range(4):
        for l in (1, 2, 3):
            panel_copy(k, l).wait_recv()
        gathered(0, gram, k)

    for first in (0, 2):
        square = jnp.zeros((2 * s, m), jnp.float32)
        for l in range(4):
            square += jnp.dot(
                panel[l, first : first + 2].reshape(2 * s, m),
                gram[l].reshape(m, m),
                preferred_element_type=jnp.float32,
            )
        for k in (first, first + 1):
            own = panel[0, k].astype(jnp.float32)
            rows = square[(k - first) * s : (k - first + 1) * s]
            poly[k, r] = (QUINTIC_B * own + QUINTIC_C * rows).astype(jnp.bfloat16)
            spread(1, poly, k)
    for d in range(1, depth):
        for k in range(4):
            pass_on(1, poly, k, d)
    for k in range(4):
        gathered(1, poly, k)
        pltpu.make_async_copy(poly.at[k], poly_out.at[k], out_sem.at[4 + k]).start()

    for k in range(4):
        if k > 1:
            pair_copy(k).wait_send()
        for d in range(1, depth):
            sum_copy(k, d).wait_send()
        for l in (1, 2, 3):
            panel_copy(k, l).wait_send()
        spread_sent(0, gram, k)
        spread_sent(1, poly, k)
        keep(k).wait()
        pltpu.make_async_copy(poly.at[k], poly_out.at[k], out_sem.at[4 + k]).wait()


def square_of_four(rows, iterate):
    m, n = iterate.shape
    depth, s = rows // 2, m // rows
    bf16, f32, dma = jnp.bfloat16, jnp.float32, pltpu.SemaphoreType.DMA
    slab, poly = pl.pallas_call(
        functools.partial(polynomial_kernel, depth, 1.0 / N),
        out_shape=(
            jax.ShapeDtypeStruct((4, m, n), bf16),
            jax.ShapeDtypeStruct((4, rows, s, m), bf16),
        ),
        in_specs=[pl.BlockSpec(memory_space=pltpu.VMEM)],
        out_specs=(pl.BlockSpec(memory_space=pl.ANY), pl.BlockSpec(memory_space=pl.ANY)),
        scratch_shapes=[
            pltpu.VMEM((3, m, n), bf16),
            pltpu.VMEM((2, 2, depth, s, m), f32),
            pltpu.VMEM((4, depth, s, m), f32),
            pltpu.VMEM((4, depth, s, m), bf16),
            pltpu.VMEM((4, depth - 1, s, m), bf16),
            pltpu.VMEM((4, rows, s, m), bf16),
            pltpu.VMEM((4, 4, s, m), bf16),
            pltpu.VMEM((4, rows, s, m), bf16),
            dma((6,)), dma((6,)),
            dma((4,)), dma((4,)),
            dma((4, depth - 1)), dma((4, depth - 1)),
            dma((2, 4, 2, depth - 1)), dma((2, 4, 2, depth - 1)),
            dma((2, 4, rows - 1)), dma((2, 4, rows - 1)),
            dma((4, 3)), dma((4, 3)),
            dma((8,)),
        ],
        compiler_params=pltpu.CompilerParams(
            collective_id=0, has_side_effects=True, vmem_limit_bytes=VMEM_LIMIT
        ),
    )(iterate)
    product = lax.dot_general(
        poly.reshape(4 * m, m), slab.reshape(4 * m, n), COLS_BY_ROWS, preferred_element_type=f32
    )
    return QUINTIC_A * iterate.astype(f32) + product


def solution(mesh):
    rows, cols = mesh.shape["row"], mesh.shape["col"]
    placed = (P("col", "row"),)

    def local(iterate):
        m, n = iterate.shape
        if cols == 4 and rows % 2 == 0 and m % (16 * rows) == 0 and 30 * m * m + 10 * m * n < VMEM_LIMIT:
            return square_of_four(rows, iterate)
        return general(iterate)

    return jax.shard_map(
        local, mesh=mesh, in_specs=placed, out_specs=P("col", "row"), check_vma=False
    )
```

time: 537 us -> 288 us (0.54)
  waiting for transfers between devices: 467 us -> 0 us
  Pallas kernels: 0 us -> 266 us
  matrix products: 53.4 us -> 22.5 us
  between operations: 13.1 us -> 0.01 us
    all_gather x4 -> x0, waiting for transfers between devices: 334 us -> none  [the longest x1 160 us: local(): column_slab = lax.all_gather(iterate, 'col', axis=0, tiled=True)]
    pallas_call x0 -> x1, Pallas kernels: none -> 266 us  [square_of_four(): pl.pallas_call(functools.partial(polynomial_kernel, depth, 1.0 / N), out_...]
    reduce_scatter x1 -> x0, waiting for transfers between devices: 132 us -> none  [local(): lax.psum_scatter(lax.dot_general(column_slab, iterate, (((1,), (1,)), (()...]
    dot_general x3 -> x1, matrix products: 53.4 us -> 22.5 us  [square_of_four(): lax.dot_general(poly.reshape(4 * m, m), slab.reshape(4 * m, n), COLS_BY_R...]
  transfers between devices with their start and end apart: 5 -> 0, of which waited for: 5 -> 0; matrix products, arithmetic and copies ran while one was open for 0% -> 0% of each run, Pallas kernels for 0% -> 0%
where the time goes in v1:
time: 288 us
  Pallas kernels  266 us (92%)
  matrix products  22.5 us (8%)
    pallas_call x1, Pallas kernels, square_of_four(): pl.pallas_call(functools.partial(polynomial_kernel, depth, 1.0 / N), out_...  266 us
    dot_general x1, matrix products, square_of_four(): lax.dot_general(poly.reshape(4 * m, m), slab.reshape(4 * m, n), COLS_BY_R...  22.5 us

profile of v1, /device:TPU:0, one launch (start us, length us, event | category | flops | bytes accessed | tf_op | source)
XLA Modules:
  0.0 288.1 jit_solution(14395131868031312130)
XLA Ops:
  0.0 265.6 %shard_map.17 = (bf16[4,896,2304]{2,1,0:T(8,128)(2,1)}, bf16[4,8,112,896]{3,2,1,0:T(8,128)(2,1)}) custom-call(bf16[896,2304]{1,0:T(8,128)(2,1)} %x_ref.1), custom_call_target="tpu_custom_call" | custom-call | tf_op jit(solution)/shard_map/pallas_call | solution.py:306
  265.6 22.5 %multiply_add_fusion = f32[896,2304]{1,0:T(8,128)} fusion(bf16[896,2304]{1,0:T(8,128)(2,1)} %x_ref.1, bf16[3584,896]{1,0:T(8,128)(2,1)} %bitcast.5, bf16[3584,2304]{1,0:T(8,128)(2,1)} %bitcast.4), kind=kOutput, calls=%fused_computation | convolution fusion | flops 14803697664 | bytes 35323904 | tf_op jit(solution)/shard_map/dot_general | solution.py:335

commit v2 on v1

--- a/solution.py
+++ b/solution.py
@@ -49,9 +49,9 @@
 
 def polynomial_kernel(
     depth, inverse, x_ref, slab_out, poly_out,
-    slab, part, paired, outgoing, incoming, gram, panel, poly,
+    slab, part, paired, outgoing, incoming, turned, gram, panel, poly,
     x_send, x_recv, pair_send, pair_recv, sum_send, sum_recv,
-    hop_send, hop_recv, side_send, side_recv, panel_send, panel_recv, out_sem,
+    hop_send, hop_recv, side_send, side_recv, panel_send, panel_recv, turn_sem, out_sem,
 ):
     m = x_ref.shape[0]
     h, s = m // 2, m // (2 * depth)
@@ -103,9 +103,10 @@
     def products(k):
         def step(i, carry):
             rows = pl.ds(pl.multiple_of(i * 2 * s, 2 * s), 2 * s)
-            block = x_ref[rows] if k == 0 else slab[k - 1, rows]
+            block = x_ref[rows] if k == 0 else slab[k - 1 if k < 3 else 0, rows]
+            other = x_ref[...] if k < 3 else slab[1]
             total = inverse * lax.dot_general(
-                block, x_ref[...], ROWS_BY_ROWS, preferred_element_type=jnp.float32
+                block, other, ROWS_BY_ROWS, preferred_element_type=jnp.float32
             )
             part[k % 2, 0, i] = total[:s]
             part[k % 2, 1, i] = total[s:]
@@ -125,7 +126,9 @@
         pair_copy(k).wait_recv()
 
         def step(i, carry):
-            outgoing[k, i] = (part[k % 2, core, i] + paired[k, i]).astype(jnp.bfloat16)
+            total = part[k % 2, core, i] + paired[k, i]
+            paired[k, i] = total
+            outgoing[k, i] = total.astype(jnp.bfloat16)
             return carry
 
         lax.fori_loop(0, depth, step, 0)
@@ -139,13 +142,23 @@
         )
 
     def finish_sums(k):
-        total = part[k % 2, core, z] + paired[k, z]
+        total = paired[k, z]
         for d in range(1, depth):
             sum_copy(k, d).wait_recv()
             total += incoming[k, d - 1].astype(jnp.float32)
         total = total.astype(jnp.bfloat16)
-        gram[k, r] = total
-        panel[0, k] = total
+        if k < 3:
+            gram[k, r] = total
+            share(k)
+        else:
+            turned[...] = total
+            turn_copy().start()
+
+    def turn_copy():
+        return remote(turned, gram.at[3, r], turn_sem.at[0], turn_sem.at[1], col=across[2])
+
+    def share(k):
+        panel[0, k] = gram[k, r]
         spread(0, gram, k)
         for l in (1, 2, 3):
             panel_copy(k, l).start()
@@ -238,32 +251,35 @@
         pass_on(0, gram, 0, d)
     for i in (2, 3):
         x_copy(i).wait()
-    x_copy(4).start()
-    x_copy(5).start()
     keep(1).start()
     keep(2).start()
     products(1)
+    send_sums(1)
     pair_copy(0).wait_send()
     products(2)
-    send_sums(1)
     send_sums(2)
+    pair_copy(1).wait_send()
+    products(3)
     finish_sums(1)
+    send_sums(3)
+    pass_on(0, gram, 1, 1)
     finish_sums(2)
-    for d in range(1, depth):
+    for d in range(2, depth):
         pass_on(0, gram, 1, d)
+    pass_on(0, gram, 2, 1)
+    finish_sums(3)
+    for d in range(2, depth):
         pass_on(0, gram, 2, d)
-    pair_copy(1).wait_send()
-    for i in (4, 5):
-        x_copy(i).wait()
-    keep(3).start()
-    products(3)
-    send_sums(3)
-    finish_sums(3)
+    turn_copy().wait()
+    share(3)
     for d in range(1, depth):
         pass_on(0, gram, 3, d)
     for k in range(4):
         for l in (1, 2, 3):
             panel_copy(k, l).wait_recv()
+    x_copy(4).start()
+    x_copy(5).start()
+    for k in range(4):
         gathered(0, gram, k)
 
     for first in (0, 2):
@@ -282,6 +298,9 @@
     for d in range(1, depth):
         for k in range(4):
             pass_on(1, poly, k, d)
+    for i in (4, 5):
+        x_copy(i).wait()
+    keep(3).start()
     for k in range(4):
         gathered(1, poly, k)
         pltpu.make_async_copy(poly.at[k], poly_out.at[k], out_sem.at[4 + k]).start()
@@ -317,6 +336,7 @@
             pltpu.VMEM((4, depth, s, m), f32),
             pltpu.VMEM((4, depth, s, m), bf16),
             pltpu.VMEM((4, depth - 1, s, m), bf16),
+            pltpu.VMEM((s, m), bf16),
             pltpu.VMEM((4, rows, s, m), bf16),
             pltpu.VMEM((4, 4, s, m), bf16),
             pltpu.VMEM((4, rows, s, m), bf16),
@@ -326,6 +346,7 @@
             dma((2, 4, 2, depth - 1)), dma((2, 4, 2, depth - 1)),
             dma((2, 4, rows - 1)), dma((2, 4, rows - 1)),
             dma((4, 3)), dma((4, 3)),
+            dma((2,)),
             dma((8,)),
         ],
         compiler_params=pltpu.CompilerParams(

time: 288 us -> 279 us (0.969)
  Pallas kernels: 266 us -> 256 us
    pallas_call x1, Pallas kernels: 266 us -> 256 us  [square_of_four(): pl.pallas_call(functools.partial(polynomial_kernel, depth, 1.0 / N), out_...]
where the time goes in v2:
time: 279 us
  Pallas kernels  256 us (92%)
  matrix products  22.5 us (8%)
    pallas_call x1, Pallas kernels, square_of_four(): pl.pallas_call(functools.partial(polynomial_kernel, depth, 1.0 / N), out_...  256 us
    dot_general x1, matrix products, square_of_four(): lax.dot_general(poly.reshape(4 * m, m), slab.reshape(4 * m, n), COLS_BY_R...  22.5 us

profile of v2, /device:TPU:0, one launch (start us, length us, event | category | flops | bytes accessed | tf_op | source)
XLA Modules:
  0.0 279.0 jit_solution(984227941425907120)
XLA Ops:
  0.0 256.5 %shard_map.17 = (bf16[4,896,2304]{2,1,0:T(8,128)(2,1)}, bf16[4,8,112,896]{3,2,1,0:T(8,128)(2,1)}) custom-call(bf16[896,2304]{1,0:T(8,128)(2,1)} %x_ref.1), custom_call_target="tpu_custom_call" | custom-call | tf_op jit(solution)/shard_map/pallas_call | solution.py:325
  256.5 22.5 %multiply_add_fusion = f32[896,2304]{1,0:T(8,128)} fusion(bf16[896,2304]{1,0:T(8,128)(2,1)} %x_ref.1, bf16[3584,896]{1,0:T(8,128)(2,1)} %bitcast.5, bf16[3584,2304]{1,0:T(8,128)(2,1)} %bitcast.4), kind=kOutput, calls=%fused_computation | convolution fusion | flops 14803697664 | bytes 35323904 | tf_op jit(solution)/shard_map/dot_general | solution.py:356

commit v3 on v2

--- a/solution.py
+++ b/solution.py
@@ -14,7 +14,7 @@
 QUINTIC_B = -4.775
 QUINTIC_C = 2.0315
 
-VMEM_LIMIT = 60 * 2**20
+VMEM_LIMIT = 63 * 2**20
 ROWS_BY_ROWS = (((1,), (1,)), ((), ()))
 COLS_BY_ROWS = (((0,), (0,)), ((), ()))
 
@@ -48,8 +48,8 @@
 
 
 def polynomial_kernel(
-    depth, inverse, x_ref, slab_out, poly_out,
-    slab, part, paired, outgoing, incoming, turned, gram, panel, poly,
+    depth, inverse, x_ref, slab_out, poly_out, total_out,
+    slab, total, part, paired, outgoing, incoming, turned, gram, panel, poly,
     x_send, x_recv, pair_send, pair_recv, sum_send, sum_recv,
     hop_send, hop_recv, side_send, side_recv, panel_send, panel_recv, turn_sem, out_sem,
 ):
@@ -91,9 +91,27 @@
             source.at[half], slab.at[block, half], x_send.at[i], x_recv.at[i], col=across[bit]
         )
 
-    def keep(k):
+    def keep(i):
+        source = (slab.at[2], poly.at[3], total)[i]
+        return pltpu.make_async_copy(source, (slab_out, poly_out, total_out)[i], out_sem.at[i])
+
+    def product(k):
         source = x_ref if k == 0 else slab.at[k - 1]
-        return pltpu.make_async_copy(source, slab_out.at[k], out_sem.at[k])
+        width = 256 if source.shape[1] % 256 == 0 else source.shape[1]
+        outgoing[0:2] = poly[k].reshape(m, m).T.reshape(2, depth, s, m)
+
+        def step(i, carry):
+            columns = pl.ds(pl.multiple_of(i * width, width), width)
+            term = jnp.dot(
+                outgoing[0:2].reshape(m, m), source[:, columns], preferred_element_type=jnp.float32
+            )
+            if k == 0:
+                total[:, columns] = QUINTIC_A * x_ref[:, columns].astype(jnp.float32) + term
+            else:
+                total[:, columns] += term
+            return carry
+
+        lax.fori_loop(0, source.shape[1] // width, step, 0)
 
     def pair_copy(k):
         return remote(
@@ -105,11 +123,11 @@
             rows = pl.ds(pl.multiple_of(i * 2 * s, 2 * s), 2 * s)
             block = x_ref[rows] if k == 0 else slab[k - 1 if k < 3 else 0, rows]
             other = x_ref[...] if k < 3 else slab[1]
-            total = inverse * lax.dot_general(
+            block_sum = inverse * lax.dot_general(
                 block, other, ROWS_BY_ROWS, preferred_element_type=jnp.float32
             )
-            part[k % 2, 0, i] = total[:s]
-            part[k % 2, 1, i] = total[s:]
+            part[k % 2, 0, i] = block_sum[:s]
+            part[k % 2, 1, i] = block_sum[s:]
             return carry
 
         lax.fori_loop(0, depth, step, 0)
@@ -126,9 +144,9 @@
         pair_copy(k).wait_recv()
 
         def step(i, carry):
-            total = part[k % 2, core, i] + paired[k, i]
-            paired[k, i] = total
-            outgoing[k, i] = total.astype(jnp.bfloat16)
+            block_sum = part[k % 2, core, i] + paired[k, i]
+            paired[k, i] = block_sum
+            outgoing[k, i] = block_sum.astype(jnp.bfloat16)
             return carry
 
         lax.fori_loop(0, depth, step, 0)
@@ -142,16 +160,16 @@
         )
 
     def finish_sums(k):
-        total = paired[k, z]
+        tile = paired[k, z]
         for d in range(1, depth):
             sum_copy(k, d).wait_recv()
-            total += incoming[k, d - 1].astype(jnp.float32)
-        total = total.astype(jnp.bfloat16)
+            tile += incoming[k, d - 1].astype(jnp.float32)
+        tile = tile.astype(jnp.bfloat16)
         if k < 3:
-            gram[k, r] = total
+            gram[k, r] = tile
             share(k)
         else:
-            turned[...] = total
+            turned[...] = tile
             turn_copy().start()
 
     def turn_copy():
@@ -239,7 +257,6 @@
 
     x_copy(0).start()
     x_copy(1).start()
-    keep(0).start()
     products(0)
     send_sums(0)
     for i in (0, 1):
@@ -251,8 +268,6 @@
         pass_on(0, gram, 0, d)
     for i in (2, 3):
         x_copy(i).wait()
-    keep(1).start()
-    keep(2).start()
     products(1)
     send_sums(1)
     pair_copy(0).wait_send()
@@ -295,43 +310,52 @@
             rows = square[(k - first) * s : (k - first + 1) * s]
             poly[k, r] = (QUINTIC_B * own + QUINTIC_C * rows).astype(jnp.bfloat16)
             spread(1, poly, k)
-    for d in range(1, depth):
-        for k in range(4):
-            pass_on(1, poly, k, d)
+    for k in range(4):
+        for d in range(1, depth):
+            sum_copy(k, d).wait_send()
+    last = depth - 1
+    for wave in range(1, 4 + last):
+        for d in range(last, 0, -1):
+            if 0 <= wave - d < 4:
+                pass_on(1, poly, wave - d, d)
+        k = wave - last - 1
+        if 0 <= k < 3:
+            gathered(1, poly, k)
+            product(k)
+    keep(2).start()
     for i in (4, 5):
         x_copy(i).wait()
-    keep(3).start()
-    for k in range(4):
-        gathered(1, poly, k)
-        pltpu.make_async_copy(poly.at[k], poly_out.at[k], out_sem.at[4 + k]).start()
+    keep(0).start()
+    gathered(1, poly, 3)
+    keep(1).start()
 
     for k in range(4):
         if k > 1:
             pair_copy(k).wait_send()
-        for d in range(1, depth):
-            sum_copy(k, d).wait_send()
         for l in (1, 2, 3):
             panel_copy(k, l).wait_send()
         spread_sent(0, gram, k)
         spread_sent(1, poly, k)
-        keep(k).wait()
-        pltpu.make_async_copy(poly.at[k], poly_out.at[k], out_sem.at[4 + k]).wait()
+    for i in range(3):
+        keep(i).wait()
 
 
 def square_of_four(rows, iterate):
     m, n = iterate.shape
     depth, s = rows // 2, m // rows
     bf16, f32, dma = jnp.bfloat16, jnp.float32, pltpu.SemaphoreType.DMA
-    slab, poly = pl.pallas_call(
+    slab, poly, total = pl.pallas_call(
         functools.partial(polynomial_kernel, depth, 1.0 / N),
         out_shape=(
-            jax.ShapeDtypeStruct((4, m, n), bf16),
-            jax.ShapeDtypeStruct((4, rows, s, m), bf16),
+            jax.ShapeDtypeStruct((m, n), bf16),
+            jax.ShapeDtypeStruct((rows, s, m), bf16),
+            jax.ShapeDtypeStruct((m, n), f32),
         ),
         in_specs=[pl.BlockSpec(memory_space=pltpu.VMEM)],
-        out_specs=(pl.BlockSpec(memory_space=pl.ANY), pl.BlockSpec(memory_space=pl.ANY)),
+        out_specs=(pl.BlockSpec(memory_space=pl.ANY),) * 3,
         scratch_shapes=[
             pltpu.VMEM((3, m, n), bf16),
+            pltpu.VMEM((m, n), f32),
             pltpu.VMEM((2, 2, depth, s, m), f32),
             pltpu.VMEM((4, depth, s, m), f32),
             pltpu.VMEM((4, depth, s, m), bf16),
@@ -347,16 +371,14 @@
             dma((2, 4, rows - 1)), dma((2, 4, rows - 1)),
             dma((4, 3)), dma((4, 3)),
             dma((2,)),
-            dma((8,)),
+            dma((3,)),
         ],
         compiler_params=pltpu.CompilerParams(
             collective_id=0, has_side_effects=True, vmem_limit_bytes=VMEM_LIMIT
         ),
     )(iterate)
-    product = lax.dot_general(
-        poly.reshape(4 * m, m), slab.reshape(4 * m, n), COLS_BY_ROWS, preferred_element_type=f32
-    )
-    return QUINTIC_A * iterate.astype(f32) + product
+    product = lax.dot_general(poly.reshape(m, m), slab, COLS_BY_ROWS, preferred_element_type=f32)
+    return total + product
 
 
 def solution(mesh):
@@ -365,7 +387,7 @@
 
     def local(iterate):
         m, n = iterate.shape
-        if cols == 4 and rows % 2 == 0 and m % (16 * rows) == 0 and 30 * m * m + 10 * m * n < VMEM_LIMIT:
+        if cols == 4 and rows % 2 == 0 and m % (16 * rows) == 0 and 43 * m * m + 12 * m * n < VMEM_LIMIT:
             return square_of_four(rows, iterate)
         return general(iterate)
 

time: 279 us -> 281 us (level)
  Pallas kernels: 256 us -> 268 us
  matrix products: 22.5 us -> 12.9 us
    pallas_call x1, Pallas kernels: 256 us -> 268 us  [square_of_four(): pl.pallas_call(functools.partial(polynomial_kernel, depth, 1.0 / N), out_...]
    dot_general x1, matrix products: 22.5 us -> 12.9 us  [square_of_four(): lax.dot_general(poly.reshape(m, m), slab, COLS_BY_ROWS, preferred_element...]
where the time goes in v3:
time: 281 us
  Pallas kernels  268 us (95%)
  matrix products  12.9 us (5%)
    pallas_call x1, Pallas kernels, square_of_four(): pl.pallas_call(functools.partial(polynomial_kernel, depth, 1.0 / N), out_...  268 us
    dot_general x1, matrix products, square_of_four(): lax.dot_general(poly.reshape(m, m), slab, COLS_BY_ROWS, preferred_element...  12.9 us

profile of v3, /device:TPU:0, one launch (start us, length us, event | category | flops | bytes accessed | tf_op | source)
XLA Modules:
  0.0 280.9 jit_solution(15587699649385424496)
XLA Ops:
  0.0 268.0 %shard_map.17 = (bf16[896,2304]{1,0:T(8,128)(2,1)}, bf16[8,112,896]{2,1,0:T(8,128)(2,1)}, f32[896,2304]{1,0:T(8,128)}) custom-call(bf16[896,2304]{1,0:T(8,128)(2,1)} %x_ref.1), custom_call_target="tpu_custom_call" | custom-call | tf_op jit(solution)/shard_map/pallas_call | solution.py:347
  268.0 12.9 %convolution_add_fusion = f32[896,2304]{1,0:T(8,128)} fusion(f32[896,2304]{1,0:T(8,128)} %get-tuple-element.8, bf16[896,896]{1,0:T(8,128)(2,1)} %bitcast.3, bf16[896,2304]{1,0:T(8,128)(2,1)} %get-tuple-element.10), kind=kOutput, calls=%fused_computation | convolution fusion | flops 3701440512 | bytes 22249472 | tf_op jit(solution)/shard_map/dot_general | solution.py:380
